TPU v7x, 512 devices: a whole 4x8x8 slice. The times are simulated.
512 devices in a mesh: rows: 8 (over z_lo, core), vec: 64 (over x, y, z_hi).
Axes of the slice: x: 4, y: 8, z: 8 (z_hi: 2, z_lo: 4; z = z_hi * 4 + z_lo), core: 2. Of those that a mesh axis runs over, the one named last changes fastest.
Arguments:
- vectors: float32 [512, 32768], P('vec', 'rows'), may hold values from -6 to 6
- tile_table: float32 [16, 128, 128], replicated, may hold values from -0.3125 to 0.3125
- offsets: int32 [256, 3], P('rows'), may hold values from -2 to 2, as said below
- tile_ids: int32 [256, 3], P('rows'), may hold values from 0 to 15
- bounds: float32 [3], replicated, may hold values from -1.9 to 2.3, as said below
Outputs:
- filtered: float32 [512, 32768], P('vec', 'rows')
- gram_matrix: float32 [512, 512], P(('rows', 'vec'))
Inputs may be any that keep to these rules, and one draw needn't show every extreme that they name: offsets[j, 0] is 0 for every row block j; wherever offsets[j, s] = o is not 0 and j + o lies in 0..255, row block j + o has a slot with offset -o and the same tile number, so the Hamiltonian is symmetric. bounds[0] < bounds[1] < bounds[2]; bounds[1] - bounds[0] lies between 0.1 and 0.3, bounds[2] - bounds[1] between 3.0 and 3.6, and bounds[1] + bounds[2] between 0.4 and 1.0.
All inputs are finite; a program needn't handle non-finite values.
Results may differ from a plain program's by a relative error of at most 0.00013.
Values sent between devices are 32-bit elements; how exact they have to be, the bound alone decides.
No kernel may reach another device: no remote copies, remote signals or barrier semaphores. Data moves between devices by JAX's collectives and lax.ppermute only.
A program may use at most 64 MiB of HBM per device.

v0:
```python
import jax
import jax.numpy as jnp
from jax import lax
from jax.sharding import PartitionSpec as P

BLOCK = 128
R = 2
STEPS = 4


def extended_2(array, sides, width):
    for axis, dim in sides:
        size, length = (lax.axis_size(axis), array.shape[dim])
        up = [(i, (i + 1) % size) for i in range(size - 1)]
        down = [(j, i) for i, j in up]
        last = lax.slice_in_dim(array, length - width, length, axis=dim)
        first = lax.slice_in_dim(array, 0, width, axis=dim)
        before = lax.ppermute(last, axis, up)
        after = lax.ppermute(first, axis, down)
        array = jnp.concatenate([before, array, after], axis=dim)
    return array


def band_product(extended, variant_table, metadata, first_block, out_blocks):
    ext_width = extended.shape[0]
    distinct = variant_table.shape[0] // 3
    slot_count = metadata.shape[1] // 2
    block_shift = metadata[first_block : first_block + out_blocks, :slot_count]
    tile_choice = metadata[first_block : first_block + out_blocks, slot_count:]
    tile_kind = jnp.where(block_shift > 0, 0, jnp.where(block_shift < 0, 1, 2)).astype(jnp.int32)
    table_index = tile_choice + distinct * tile_kind
    positions = first_block + jnp.arange(out_blocks, dtype=jnp.int32)
    sources = positions[:, None] + block_shift
    inside = ((sources >= 0) & (sources < ext_width)).astype(jnp.float32)
    clipped = jnp.clip(sources, 0, ext_width - 1)
    group_size = 8

    def one_group(group_items):
        source_index, keep_mask, tile_index = group_items
        incoming_block = extended[source_index] * keep_mask[:, :, None, None]
        selected_entry = variant_table[tile_index]
        return jnp.einsum(
            "gskc,gsdc->gkd",
            incoming_block,
            selected_entry,
            precision=lax.Precision.HIGHEST,
            preferred_element_type=jnp.float32,
        )

    grouped = lax.map(
        one_group,
        (
            clipped.reshape(-1, group_size, slot_count),
            inside.reshape(-1, group_size, slot_count),
            table_index.reshape(-1, group_size, slot_count),
        ),
    )
    return grouped.reshape((out_blocks,) + extended.shape[1:])


def chebyshev(blocks, operate, bounds):
    half_width = (bounds[2] - bounds[1]) / 2
    centre = (bounds[2] + bounds[1]) / 2
    sigma_one = half_width / (bounds[0] - centre)
    sigma_base = 2 / sigma_one
    previous = blocks
    present_vectors = sigma_one / half_width * (operate(blocks) - centre * blocks)
    sigma_now = sigma_one
    for repeat in range(STEPS - 1):
        sigma_next = 1 / (sigma_base - sigma_now)
        advanced = (
            2 * sigma_next / half_width * (operate(present_vectors) - centre * present_vectors)
            - sigma_now * sigma_next * previous
        )
        previous = present_vectors
        present_vectors = advanced
        sigma_now = sigma_next
    return present_vectors


def on_device(vectors, tile_table, offsets, tile_ids, bounds):
    local_vecs = vectors.shape[0]
    local_rows = vectors.shape[1]
    block_count = local_rows // BLOCK
    blocks = vectors.reshape(local_vecs, block_count, BLOCK).transpose(1, 0, 2)
    metadata = jnp.concatenate([offsets, tile_ids], axis=1)
    flipped = tile_table.transpose(0, 2, 1)
    variant_table = jnp.concatenate([tile_table, flipped, (tile_table + flipped) / 2], axis=0)
    padded_meta = jnp.pad(metadata, ((R, R), (0, 0)))

    def apply_locally(field):
        padded = extended_2(field, (("rows", 0),), R)
        return band_product(padded, variant_table, padded_meta, R, block_count)

    filtered_blocks = chebyshev(blocks, apply_locally, bounds)
    filtered = filtered_blocks.transpose(1, 0, 2).reshape(local_vecs, local_rows)
    stacked = lax.all_to_all(filtered, "vec", split_axis=1, concat_axis=0, tiled=True)
    total_vecs = stacked.shape[0]
    all_rows = local_rows * lax.axis_size("rows")
    owner_count = lax.axis_size(("rows", "vec"))
    owned_rows = total_vecs // owner_count
    contract = (((1,), (1,)), ((), ()))
    partial_value = (
        lax.dot_general(
            stacked,
            stacked,
            contract,
            precision=lax.Precision.HIGHEST,
            preferred_element_type=jnp.float32,
        )
        / all_rows
    )
    summed_gram = lax.psum(partial_value, ("rows", "vec"))
    gram_matrix = lax.dynamic_slice_in_dim(
        summed_gram, lax.axis_index(("rows", "vec")) * owned_rows, owned_rows, 0
    )
    return (filtered, gram_matrix)


def solution(mesh):
    placed = (P("vec", "rows"), P(), P("rows", None), P("rows", None), P())
    return jax.shard_map(
        on_device,
        mesh=mesh,
        in_specs=placed,
        out_specs=(P("vec", "rows"), P(("rows", "vec"), None)),
        check_vma=False,
    )
```

profile of v0, /device:TPU:24, one launch (start us, length us, event | category | flops | bytes accessed | tf_op | source)
XLA Modules:
  0.0 477.2 jit_solution(14210082805207283505)
XLA Ops:
  7.2 0.8 fusion.23
  8.0 1.7 collective-permute-start
  9.8 1.3 collective-permute-start.1
  11.1 1.6 copy.55
  12.8 0.8 copy-done.2
  14.3 1.6 pad_maximum_fusion
  15.9 0.7 fusion.24
  20.9 26.8 %while.40 = (s32[]{:T(128)}, f32[4,8,8,128]{3,2,1,0:T(8,128)}, s32[4,8,3]{1,0,2:T(4,128)S(1)}, f32[36,8,128]{2,1,0:T(8,128)S(1)}, f32[4,8,3]{1,2,0:T(4,128)S(1)}...) while((s32[]{:T(128)}, f32[4,8,8,128]{3,2,1,0:T(8,128)}, s32[4,8,3]{1,0,2:T(4,128)S(1)}, ...), condition=%wide.region_1.2_spmd, body=%wide.region_0.1_spmd.sunk | while | flops 37775504 | bytes 5057085 | solution.py:50
  21.1 1.8 gather_fusion
  23.8 3.8 fusion.44
  27.8 1.8 gather_fusion
  30.5 3.8 fusion.44
  34.5 1.8 gather_fusion
  37.2 3.8 fusion.44
  41.2 1.8 gather_fusion
  43.9 3.8 fusion.44
  47.7 0.9 fusion.19
  49.3 5.2 %collective-permute-start.2 = (f32[2,8,128]{2,1,0:T(8,128)S(1)}, f32[2,8,128]{2,1,0:T(8,128)S(1)}, u32[]{:S(2)}, u32[]{:S(2)}) collective-permute-start(f32[2,8,128]{2,1,0:T(8,128)S(1)} %get-tuple-element.306), channel_id=1, source_target_pairs={{0,64},{64,128},{128,192},{192,256},{256,320},{320,384},{384,448},... | collective-permute-start | bytes 24584 | tf_op jit(solution)/shard_map/ppermute | solution.py:18
  54.4 1.3 collective-permute-start.3
  55.9 2.8 collective-permute-done.3
  58.8 0.9 pad_maximum_fusion.2
  60.3 26.8 %while.41 = (s32[]{:T(128)}, f32[4,8,8,128]{3,2,1,0:T(8,128)}, s32[4,8,3]{1,0,2:T(4,128)S(1)}, f32[36,8,128]{2,1,0:T(8,128)S(1)}, f32[4,8,3]{1,2,0:T(4,128)S(1)}...) while((s32[]{:T(128)}, f32[4,8,8,128]{3,2,1,0:T(8,128)}, s32[4,8,3]{1,0,2:T(4,128)S(1)}, ...), condition=%wide.region_3.4_spmd, body=%wide.region_2.3_spmd.sunk | while | flops 37775504 | bytes 5057085 | solution.py:50
  60.5 1.8 gather_fusion.2
  63.2 3.8 fusion.47
  67.2 1.8 gather_fusion.2
  69.9 3.8 fusion.47
  73.9 1.8 gather_fusion.2
  76.6 3.8 fusion.47
  80.6 1.8 gather_fusion.2
  83.3 3.8 fusion.47
  87.2 1.0 fusion.18
  88.8 4.3 collective-permute-start.4
  93.1 1.3 collective-permute-start.5
  94.5 1.7 collective-permute-done.5
  96.2 0.9 pad_maximum_fusion.3
  97.8 26.8 %while.42 = (s32[]{:T(128)}, f32[4,8,8,128]{3,2,1,0:T(8,128)}, s32[4,8,3]{1,0,2:T(4,128)S(1)}, f32[36,8,128]{2,1,0:T(8,128)S(1)}, f32[4,8,3]{1,2,0:T(4,128)S(1)}...) while((s32[]{:T(128)}, f32[4,8,8,128]{3,2,1,0:T(8,128)}, s32[4,8,3]{1,0,2:T(4,128)S(1)}, ...), condition=%wide.region_5.6_spmd, body=%wide.region_4.5_spmd.sunk | while | flops 37775504 | bytes 5057085 | solution.py:50
  98.0 1.8 gather_fusion.4
  100.7 3.8 fusion.50
  104.7 1.8 gather_fusion.4
  107.4 3.8 fusion.50
  111.4 1.8 gather_fusion.4
  114.1 3.8 fusion.50
  118.1 1.8 gather_fusion.4
  120.8 3.8 fusion.50
  124.6 1.1 fusion.16
  126.3 4.6 collective-permute-start.6
  130.9 1.3 collective-permute-start.7
  132.3 1.7 collective-permute-done.7
  133.9 0.9 pad_maximum_fusion.4
  135.5 26.8 %while.43 = (s32[]{:T(128)}, f32[4,8,8,128]{3,2,1,0:T(8,128)}, s32[4,8,3]{1,0,2:T(4,128)S(1)}, f32[36,8,128]{2,1,0:T(8,128)S(1)}, f32[4,8,3]{1,2,0:T(4,128)S(1)}...) while((s32[]{:T(128)}, f32[4,8,8,128]{3,2,1,0:T(8,128)}, s32[4,8,3]{1,0,2:T(4,128)S(1)}, ...), condition=%wide.region_7.8_spmd, body=%wide.region_6.7_spmd.sunk | while | flops 37775504 | bytes 5057085 | solution.py:50
  135.7 1.8 gather_fusion.6
  138.4 3.8 fusion.53
  142.4 1.8 gather_fusion.6
  145.1 3.8 fusion.53
  149.1 1.8 gather_fusion.6
  151.8 3.8 fusion.53
  155.8 1.8 gather_fusion.6
  158.5 3.8 fusion.53
  162.3 1.0 fusion.14
  163.9 30.0 %all_to_all.19 = f32[64,1,512]{2,1,0:T(1,128)S(1)} all-to-all(f32[64,1,512]{2,1,0:T(1,128)S(1)} %reshape.378), channel_id=1, replica_groups=mesh['rows'=8,'vec'=64] {'vec'}, dimensions={0} | all-to-all | bytes 262144 | tf_op jit(solution)/shard_map/all_to_all | solution.py:97
  194.3 0.9 reduce
  195.4 2.0 convolution_multiply_fusion
  197.4 271.7 %all-reduce.2.cloned.1.call-done = f32[512,512]{1,0:T(8,128)} async-done(((f32[512,512]{1,0:T(8,128)}), f32[512,512]{1,0:T(8,128)}) %all-reduce.2.cloned.1.call-update) | async-done | bytes 1048592 | tf_op jit(solution)/shard_map/psum | solution.py:113
  469.1 1.3 constant_dynamic-slice_fusion
  (212 shorter events, 23.2 us)
Async XLA Ops:
  7.2 5.5 %copy-start = (f32[16,128,128]{2,1,0:T(8,128)S(1)}, f32[16,128,128]{2,1,0:T(8,128)}, u32[]{:S(2)}) copy-start(f32[16,128,128]{2,1,0:T(8,128)} %param.14) | copy-start | bytes 3145732
  7.2 461.9 %all-reduce.2.cloned.1.call-start = ((), (), s32[]{:S(2)}) async-start(), calls=%async_computation.1 | async-start | bytes 2097152 | tf_op jit(solution)/shard_map/psum | solution.py:113
  8.0 12.2 %collective-permute-start = (f32[2,8,128]{2,1,0:T(8,128)S(1)}, f32[2,8,128]{2,1,0:T(8,128)S(1)}, u32[]{:S(2)}, u32[]{:S(2)}) collective-permute-start(f32[2,8,128]{2,1,0:T(8,128)S(1)} %get-tuple-element.308), channel_id=1, source_target_pairs={{0,64},{64,128},{128,192},{192,256},{256,320},{320,384},{384,448},... | collective-permute-start | bytes 24584 | tf_op jit(solution)/shard_map/ppermute | solution.py:18
  9.8 10.5 %collective-permute-start.1 = (f32[2,8,128]{2,1,0:T(8,128)S(1)}, f32[2,8,128]{2,1,0:T(8,128)S(1)}, u32[]{:S(2)}, u32[]{:S(2)}) collective-permute-start(f32[2,8,128]{2,1,0:T(8,128)S(1)} %get-tuple-element.309), channel_id=1, source_target_pairs={{64,0},{128,64},{192,128},{256,192},{320,256},{384,320},{448,384},... | collective-permute-start | bytes 24584 | tf_op jit(solution)/shard_map/ppermute | solution.py:19
  12.6 1.0 copy-start.2
  12.6 1.0 copy-start.9
  12.7 1.0 copy-start.11
  12.7 1.6 copy-start.1
  14.3 1.6 copy-start.10
  14.3 5.9 %copy-start.3 = (f32[8,4096]{1,0:T(8,128)S(1)}, f32[8,4096]{1,0:T(8,128)}, u32[]{:S(2)}) copy-start(f32[8,4096]{1,0:T(8,128)} %param.13) | copy-start | bytes 393220
  48.6 0.7 copy-start.7
  49.3 6.7 %collective-permute-start.2 = (f32[2,8,128]{2,1,0:T(8,128)S(1)}, f32[2,8,128]{2,1,0:T(8,128)S(1)}, u32[]{:S(2)}, u32[]{:S(2)}) collective-permute-start(f32[2,8,128]{2,1,0:T(8,128)S(1)} %get-tuple-element.306), channel_id=1, source_target_pairs={{0,64},{64,128},{128,192},{192,256},{256,320},{320,384},{384,448},... | collective-permute-start | bytes 24584 | tf_op jit(solution)/shard_map/ppermute | solution.py:18
  54.4 4.3 collective-permute-start.3
  88.2 0.7 copy-start.4
  88.8 5.7 %collective-permute-start.4 = (f32[2,8,128]{2,1,0:T(8,128)S(1)}, f32[2,8,128]{2,1,0:T(8,128)S(1)}, u32[]{:S(2)}, u32[]{:S(2)}) collective-permute-start(f32[2,8,128]{2,1,0:T(8,128)S(1)} %get-tuple-element.304), channel_id=1, source_target_pairs={{0,64},{64,128},{128,192},{192,256},{256,320},{320,384},{384,448},... | collective-permute-start | bytes 24584 | tf_op jit(solution)/shard_map/ppermute | solution.py:18
  93.1 3.1 collective-permute-start.5
  125.7 0.6 copy-start.6
  126.3 6.0 %collective-permute-start.6 = (f32[2,8,128]{2,1,0:T(8,128)S(1)}, f32[2,8,128]{2,1,0:T(8,128)S(1)}, u32[]{:S(2)}, u32[]{:S(2)}) collective-permute-start(f32[2,8,128]{2,1,0:T(8,128)S(1)} %get-tuple-element.302), channel_id=1, source_target_pairs={{0,64},{64,128},{128,192},{192,256},{256,320},{320,384},{384,448},... | collective-permute-start | bytes 24584 | tf_op jit(solution)/shard_map/ppermute | solution.py:18
  130.9 3.1 collective-permute-start.7
  135.5 26.8 %copy-start.5 = (f32[32,8,128]{2,1,0:T(8,128)S(1)}, f32[32,8,128]{2,1,0:T(8,128)}, u32[]{:S(2)}) copy-start(f32[32,8,128]{2,1,0:T(8,128)} %copy-done.4) | copy-start | bytes 393220
  163.3 34.0 %copy-start.8 = (f32[32,8,128]{2,1,0:T(8,128)}, f32[32,8,128]{2,1,0:T(8,128)S(1)}, u32[]{:S(2)}) copy-start(f32[32,8,128]{2,1,0:T(8,128)S(1)} %fusion.14) | copy-start | bytes 393220
Sparse Core Ops, SparseCore 0:
  197.5 271.5 all-reduce.1
where the time goes:
time: 478 us; the launch traced here: 477 us
  waiting for transfers between devices  278 us (58%)
  matrix products  62.9 us (13%)
  local copies, waits for them, and re-layouts  57.2 us (12%)
  blocking collectives  30 us (6%)
  starting transfers between devices  21 us (4%)
  between operations  18.1 us (4%)
  other arithmetic  9.89 us (2%)
    psum x1, waiting for transfers between devices, on_device(): summed_gram = lax.psum(partial_value, ('rows', 'vec'))  272 us
    dot_general x16, matrix products, one_group(): jnp.einsum('gskc,gsdc->gkd', incoming_block, selected_entry, precision=la...  60.9 us
    all_to_all x1, blocking collectives, on_device(): lax.all_to_all(filtered, 'vec', split_axis=1, concat_axis=0, tiled=True)  30 us
    gather x16, local copies, waits for them, and re-layouts, one_group(): selected_entry = variant_table[tile_index]  29.5 us
    ppermute x4, starting transfers between devices, extended_2(): before = lax.ppermute(last, axis, up)  15.8 us
  transfers between devices with their start and end apart: 9, of which 4 were waited for; matrix products, arithmetic and copies ran while one was open for 1% of the time, Pallas kernels for 0%

commit v1 on v0

--- a/solution.py
+++ b/solution.py
@@ -110,7 +110,8 @@
         )
         / all_rows
     )
-    summed_gram = lax.psum(partial_value, ("rows", "vec"))
+    half = lax.psum(partial_value, "rows")
+    summed_gram = lax.psum(half, "vec")
     gram_matrix = lax.dynamic_slice_in_dim(
         summed_gram, lax.axis_index(("rows", "vec")) * owned_rows, owned_rows, 0
     )

time: 478 us -> 1130 us (2.36)
  the two profiles are of different devices: /device:TPU:24 before, /device:TPU:8 now
where the time goes in v1:
time: 1130 us
  waiting for transfers between devices  932 us (82%)
  matrix products  62.9 us (6%)
  local copies, waits for them, and re-layouts  56.3 us (5%)
  blocking collectives  31.1 us (3%)
  starting transfers between devices  21 us (2%)
  between operations  18 us (2%)
    psum x1, waiting for transfers between devices, on_device(): summed_gram = lax.psum(half, 'vec')  852 us
    psum x1, waiting for transfers between devices, on_device(): half = lax.psum(partial_value, 'rows')  74.7 us
    dot_general x16, matrix products, one_group(): jnp.einsum('gskc,gsdc->gkd', incoming_block, selected_entry, precision=la...  61 us
    all_to_all x1, blocking collectives, on_device(): lax.all_to_all(filtered, 'vec', split_axis=1, concat_axis=0, tiled=True)  31.1 us
    gather x16, local copies, waits for them, and re-layouts, one_group(): selected_entry = variant_table[tile_index]  29.4 us
  transfers between devices with their start and end apart: 10, of which 5 were waited for; matrix products, arithmetic and copies ran while one was open for 0% of the time, Pallas kernels for 0%

profile of v1, /device:TPU:8, one launch (start us, length us, event | category | flops | bytes accessed | tf_op | source)
XLA Modules:
  0.0 1131.3 jit_solution(7140984587475921914)
XLA Ops:
  7.2 0.8 fusion.23
  8.0 1.7 collective-permute-start
  9.8 1.3 collective-permute-start.1
  11.1 1.6 copy.55
  12.8 0.8 copy-done.2
  14.3 1.5 pad_maximum_fusion
  20.6 26.7 %while.40 = (s32[]{:T(128)}, f32[4,8,8,128]{3,2,1,0:T(8,128)}, s32[4,8,3]{1,0,2:T(4,128)S(1)}, f32[36,8,128]{2,1,0:T(8,128)S(1)}, f32[4,8,3]{1,2,0:T(4,128)S(1)}...) while((s32[]{:T(128)}, f32[4,8,8,128]{3,2,1,0:T(8,128)}, s32[4,8,3]{1,0,2:T(4,128)S(1)}, ...), condition=%wide.region_1.2_spmd, body=%wide.region_0.1_spmd.sunk | while | flops 37775504 | bytes 5057085 | solution.py:50
  20.8 1.8 gather_fusion
  23.5 3.8 fusion.44
  27.5 1.8 gather_fusion
  30.2 3.8 fusion.44
  34.2 1.8 gather_fusion
  36.9 3.8 fusion.44
  40.9 1.8 gather_fusion
  43.6 3.8 fusion.44
  47.4 0.9 fusion.19
  48.3 5.2 collective-permute-start.2
  53.5 1.3 collective-permute-start.3
  55.6 2.4 collective-permute-done.3
  58.0 0.9 pad_maximum_fusion.2
  59.6 26.8 %while.41 = (s32[]{:T(128)}, f32[4,8,8,128]{3,2,1,0:T(8,128)}, s32[4,8,3]{1,0,2:T(4,128)S(1)}, f32[36,8,128]{2,1,0:T(8,128)S(1)}, f32[4,8,3]{1,2,0:T(4,128)S(1)}...) while((s32[]{:T(128)}, f32[4,8,8,128]{3,2,1,0:T(8,128)}, s32[4,8,3]{1,0,2:T(4,128)S(1)}, ...), condition=%wide.region_3.4_spmd, body=%wide.region_2.3_spmd.sunk | while | flops 37775504 | bytes 5057085 | solution.py:50
  59.8 1.8 gather_fusion.2
  62.5 3.8 fusion.47
  66.4 1.8 gather_fusion.2
  69.1 3.8 fusion.47
  73.1 1.8 gather_fusion.2
  75.8 3.8 fusion.47
  79.8 1.8 gather_fusion.2
  82.5 3.8 fusion.47
  86.3 1.0 fusion.18
  87.4 4.3 collective-permute-start.4
  91.7 1.3 collective-permute-start.5
  93.7 1.2 collective-permute-done.5
  94.9 0.9 pad_maximum_fusion.3
  96.5 26.8 %while.42 = (s32[]{:T(128)}, f32[4,8,8,128]{3,2,1,0:T(8,128)}, s32[4,8,3]{1,0,2:T(4,128)S(1)}, f32[36,8,128]{2,1,0:T(8,128)S(1)}, f32[4,8,3]{1,2,0:T(4,128)S(1)}...) while((s32[]{:T(128)}, f32[4,8,8,128]{3,2,1,0:T(8,128)}, s32[4,8,3]{1,0,2:T(4,128)S(1)}, ...), condition=%wide.region_5.6_spmd, body=%wide.region_4.5_spmd.sunk | while | flops 37775504 | bytes 5057085 | solution.py:50
  96.7 1.8 gather_fusion.4
  99.3 3.8 fusion.50
  103.3 1.8 gather_fusion.4
  106.0 3.8 fusion.50
  110.0 1.8 gather_fusion.4
  112.7 3.8 fusion.50
  116.7 1.8 gather_fusion.4
  119.4 3.8 fusion.50
  123.2 1.1 fusion.16
  124.3 4.5 collective-permute-start.6
  128.9 1.3 collective-permute-start.7
  130.3 1.7 collective-permute-done.7
  131.9 0.9 pad_maximum_fusion.4
  133.5 26.8 %while.43 = (s32[]{:T(128)}, f32[4,8,8,128]{3,2,1,0:T(8,128)}, s32[4,8,3]{1,0,2:T(4,128)S(1)}, f32[36,8,128]{2,1,0:T(8,128)S(1)}, f32[4,8,3]{1,2,0:T(4,128)S(1)}...) while((s32[]{:T(128)}, f32[4,8,8,128]{3,2,1,0:T(8,128)}, s32[4,8,3]{1,0,2:T(4,128)S(1)}, ...), condition=%wide.region_7.8_spmd, body=%wide.region_6.7_spmd.sunk | while | flops 37775504 | bytes 5057085 | solution.py:50
  133.7 1.8 gather_fusion.6
  136.4 3.8 fusion.53
  140.4 1.8 gather_fusion.6
  143.1 3.8 fusion.53
  147.1 1.8 gather_fusion.6
  149.8 3.8 fusion.53
  153.8 1.8 gather_fusion.6
  156.5 3.8 fusion.53
  160.3 1.0 fusion.14
  161.8 31.1 %all_to_all.19 = f32[64,1,512]{2,1,0:T(1,128)S(1)} all-to-all(f32[64,1,512]{2,1,0:T(1,128)S(1)} %reshape.378), channel_id=1, replica_groups=mesh['rows'=8,'vec'=64] {'vec'}, dimensions={0} | all-to-all | bytes 262144 | tf_op jit(solution)/shard_map/all_to_all | solution.py:97
  193.4 0.9 reduce
  194.5 2.0 convolution_multiply_fusion
  196.5 74.7 %all-reduce.3.cloned.1.call-done = f32[512,512]{1,0:T(8,128)} async-done(((f32[512,512]{1,0:T(8,128)}), f32[512,512]{1,0:T(8,128)}) %all-reduce.3.cloned.1.call-update) | async-done | bytes 1048592 | tf_op jit(solution)/shard_map/psum | solution.py:113
  271.2 851.9 %all-reduce.5.cloned.1.call-done = f32[512,512]{1,0:T(8,128)} async-done(((f32[512,512]{1,0:T(8,128)}), f32[512,512]{1,0:T(8,128)}) %all-reduce.5.cloned.1.call-update) | async-done | bytes 1048592 | tf_op jit(solution)/shard_map/psum | solution.py:114
  1123.2 1.3 constant_dynamic-slice_fusion
  (219 shorter events, 23.2 us)
Async XLA Ops:
  7.2 5.5 copy-start
  7.2 264.0 %all-reduce.3.cloned.1.call-start = ((), (), s32[]{:S(2)}) async-start(), calls=%async_computation.1 | async-start | bytes 2097152 | tf_op jit(solution)/shard_map/psum | solution.py:113
  8.0 11.9 %collective-permute-start = (f32[2,8,128]{2,1,0:T(8,128)S(1)}, f32[2,8,128]{2,1,0:T(8,128)S(1)}, u32[]{:S(2)}, u32[]{:S(2)}) collective-permute-start(f32[2,8,128]{2,1,0:T(8,128)S(1)} %get-tuple-element.308), channel_id=1, source_target_pairs={{0,64},{64,128},{128,192},{192,256},{256,320},{320,384},{384,448},... | collective-permute-start | bytes 24584 | tf_op jit(solution)/shard_map/ppermute | solution.py:18
  9.8 10.2 collective-permute-start.1
  12.6 1.0 copy-start.2
  12.6 1.0 copy-start.11
  12.7 1.0 copy-start.13
  12.7 1.6 copy-start.1
  14.3 1.5 copy-start.12
  14.3 5.7 copy-start.3
  48.3 6.7 copy-start.7
  48.3 6.7 collective-permute-start.2
  53.5 4.4 collective-permute-start.3
  55.0 0.6 copy-start.9
  87.4 5.7 copy-start.4
  87.4 5.7 collective-permute-start.4
  91.7 3.2 collective-permute-start.5
  93.1 0.6 copy-start.10
  124.3 6.0 copy-start.6
  124.3 5.9 collective-permute-start.6
  128.9 3.1 collective-permute-start.7
  133.5 26.8 %copy-start.5 = (f32[32,8,128]{2,1,0:T(8,128)S(1)}, f32[32,8,128]{2,1,0:T(8,128)}, u32[]{:S(2)}) copy-start(f32[32,8,128]{2,1,0:T(8,128)} %copy-done.4) | copy-start | bytes 393220
  161.3 35.1 %copy-start.8 = (f32[32,8,128]{2,1,0:T(8,128)}, f32[32,8,128]{2,1,0:T(8,128)S(1)}, u32[]{:S(2)}) copy-start(f32[32,8,128]{2,1,0:T(8,128)S(1)} %fusion.14) | copy-start | bytes 393220
  196.5 926.7 %all-reduce.5.cloned.1.call-start = ((), (), s32[]{:S(2)}) async-start(), calls=%async_computation.2 | async-start | bytes 2097152 | tf_op jit(solution)/shard_map/psum | solution.py:114
Sparse Core Ops, SparseCore 0:
  196.6 74.5 all-reduce.2
  274.1 849.0 all-reduce.4
